TPU v7x, 32 devices: a whole 2x2x4 slice. The times are simulated.
32 devices in a mesh: patch: 8 (over z, y), coarse: 4 (over x, core).
Axes of the slice: x: 2, y: 2, z: 4, core: 2. Of those that a mesh axis runs over, the one named last changes fastest.
Arguments:
- residual: bfloat16 [2, 2, 49152, 256], P(None, None, ('patch', 'coarse')), may hold values from -6 to 6
- patch_inv: bfloat16 [128, 2, 1024, 1024], P(('patch', 'coarse')), may hold values from -0.1875 to 0.1875
- coarse_basis: bfloat16 [128, 2, 1024, 32], P(('patch', 'coarse')), may hold values from -0.1875 to 0.1875
- coarse_inv: bfloat16 [64, 2, 32, 32], P('coarse'), may hold values from -1 to 1
- patch_slots: int32 [128, 512], P(('patch', 'coarse')), may hold values from 0 to 1791, as said below
- send_rows: int32 [32, 2, 128], P(('patch', 'coarse')), may hold values from 0 to 1535, as said below
- coarse_block: int32 [128], P(('patch', 'coarse')), may hold values from 0 to 63
Outputs:
- correction: bfloat16 [2, 2, 49152, 256], P(None, None, ('patch', 'coarse'))
Inputs may be any that keep to these rules, and one draw needn't show every extreme that they name: `send_rows`: within each of the two blocks of a device the 128 rows are distinct. `patch_slots`: the 512 positions of a patch are distinct; they hold its device's rows (p mod 4) * 384 to (p mod 4 + 1) * 384 - 1, 64 positions of 1536 or more, and other rows of its device below 1536; each position of 1536 or more is used by exactly one patch of the device.
All inputs are finite; a program needn't handle non-finite values.
Results may differ from a plain program's by a relative error of at most 0.006.
Values may be sent and summed in bfloat16 or wider, within the bound.
No kernel may reach another device: no remote copies, remote signals or barrier semaphores. Data moves between devices by JAX's collectives and lax.ppermute only.
A program may use at most 128 MiB of HBM per device.

v0:
```python
import jax
import jax.numpy as jnp
from jax import lax
from jax.sharding import PartitionSpec as P


def passed_along(value, axis, steps):
    count = lax.axis_size(axis)
    pairs = [(source, (source + steps) % count) for source in range(count)]
    return lax.ppermute(value, axis, pairs)


def spread_rows(selector, terms, form):
    upper_part = terms.astype(jnp.bfloat16)
    lower_part = (terms - upper_part.astype(jnp.float32)).astype(jnp.bfloat16)
    first = jnp.einsum(form, selector, upper_part, preferred_element_type=jnp.float32)
    return first + jnp.einsum(form, selector, lower_part, preferred_element_type=jnp.float32)


def per_device(residual, patch_inv, coarse_basis, coarse_inv, patch_slots, send_rows, coarse_block):
    wave_count = residual.shape[0]
    node_rows = residual.shape[2]
    patches = patch_inv.shape[0]
    patch_nodes = patch_inv.shape[2] // 2
    coarse_width = coarse_basis.shape[3]
    slot_rows = send_rows.shape[2]
    ext_rows = node_rows + 2 * slot_rows
    blocks_all = coarse_inv.shape[0] * lax.axis_size("coarse")
    highest = lax.Precision.HIGHEST
    node_ids = jnp.arange(node_rows, dtype=jnp.int32)
    up_select = (send_rows[0, 0][:, None] == node_ids[None, :]).astype(jnp.bfloat16)
    down_select = (send_rows[0, 1][:, None] == node_ids[None, :]).astype(jnp.bfloat16)
    upward = jnp.einsum(
        "kn,wqnr->wqkr", up_select, residual, preferred_element_type=jnp.float32
    ).astype(jnp.bfloat16)
    downward = jnp.einsum(
        "kn,wqnr->wqkr", down_select, residual, preferred_element_type=jnp.float32
    ).astype(jnp.bfloat16)
    from_below = passed_along(upward, ("patch", "coarse"), 1)
    from_above = passed_along(downward, ("patch", "coarse"), -1)
    extended = jnp.concatenate([residual, from_below, from_above], axis=2)
    ext_select = (
        patch_slots[:, :, None] == jnp.arange(ext_rows, dtype=jnp.int32)[None, None, :]
    ).astype(jnp.bfloat16)
    gathered = jnp.einsum(
        "pne,wqer->wqpnr", ext_select, extended, preferred_element_type=jnp.float32
    ).astype(jnp.bfloat16)
    basis_cols = coarse_basis.reshape(patches, wave_count, 2, patch_nodes, coarse_width)
    restricted = jnp.einsum(
        "pwqnc,wqpnr->pwcr", basis_cols, gathered, preferred_element_type=jnp.float32
    )
    member = coarse_block[:, None] == jnp.arange(blocks_all, dtype=jnp.int32)[None, :]
    partial_sums = jnp.einsum(
        "pb,pwcr->bwcr", member.astype(jnp.float32), restricted, precision=highest
    )
    totals = lax.psum(partial_sums, ("patch", "coarse"))
    inverses = lax.all_gather(coarse_inv, "coarse", axis=0, tiled=True)
    coarse_coef = jnp.einsum(
        "bwcd,bwdr->bwcr", inverses.astype(jnp.float32), totals, precision=highest
    ).astype(jnp.bfloat16)
    patch_coef = jnp.einsum(
        "pb,bwcr->pwcr",
        member.astype(jnp.bfloat16),
        coarse_coef,
        preferred_element_type=jnp.float32,
    ).astype(jnp.bfloat16)
    inverse = patch_inv.reshape(patches, wave_count, 2, patch_nodes, 2, patch_nodes)
    local_terms = jnp.einsum(
        "pwabqn,wqpnr->wapbr", inverse, gathered, preferred_element_type=jnp.float32
    )
    local_terms = local_terms + jnp.einsum(
        "pwqnc,pwcr->wqpnr", basis_cols, patch_coef, preferred_element_type=jnp.float32
    )
    collected = spread_rows(ext_select, local_terms, "pne,wqpnr->wqer")
    to_lower = collected[:, :, node_rows : node_rows + slot_rows]
    to_upper = collected[:, :, node_rows + slot_rows :]
    back_from_above = passed_along(to_lower.astype(jnp.bfloat16), ("patch", "coarse"), -1).astype(
        to_lower.dtype
    )
    back_from_below = passed_along(to_upper.astype(jnp.bfloat16), ("patch", "coarse"), 1).astype(
        to_upper.dtype
    )
    summed = collected[:, :, :node_rows]
    summed = summed + spread_rows(up_select, back_from_above, "kn,wqkr->wqnr")
    summed = summed + spread_rows(down_select, back_from_below, "kn,wqkr->wqnr")
    return summed.astype(jnp.bfloat16)


def solution(mesh):
    placed = (
        P(None, None, ("patch", "coarse"), None),
        P(("patch", "coarse"), None, None, None),
        P(("patch", "coarse"), None, None, None),
        P("coarse", None, None, None),
        P(("patch", "coarse"), None),
        P(("patch", "coarse"), None, None),
        P(("patch", "coarse")),
    )
    return jax.shard_map(
        per_device,
        mesh=mesh,
        in_specs=placed,
        out_specs=P(None, None, ("patch", "coarse"), None),
        check_vma=False,
    )
```

profile of v0, /device:TPU:0, one launch (start us, length us, event | category | flops | bytes accessed | tf_op | source)
XLA Modules:
  0.0 256.1 jit_solution(5155626987619132174)
XLA Ops:
  6.5 0.8 slice_bitcast_fusion.1
  7.4 2.6 %fusion.39 = bf16[2,2,128,256]{3,2,1,0:T(8,128)(2,1)S(1)} fusion(bf16[2,2,1536,256]{3,2,1,0:T(8,128)(2,1)} %param.7, s32[128]{0:T(128)S(1)} %get-tuple-element.7), kind=kOutput, calls=%fused_computation.37 | convolution fusion | flops 402980864 | bytes 3408384 | tf_op jit(solution)/shard_map/kn,wqnr->wqkr/dot_general | solution.py:33
  10.0 0.5 collective-permute-start
  10.6 3.2 %fusion.40 = bf16[2,2,128,256]{3,2,1,0:T(8,128)(2,1)} fusion(bf16[2,2,1536,256]{3,2,1,0:T(8,128)(2,1)} %param.7, s32[128]{0:T(128)S(1)} %get-tuple-element.8), kind=kOutput, calls=%fused_computation.38 | convolution fusion | flops 402980864 | bytes 3408384 | tf_op jit(solution)/shard_map/kn,wqnr->wqkr/dot_general | solution.py:36
  13.8 5.9 %collective-permute-start.1 = (bf16[2,2,128,256]{3,2,1,0:T(8,128)(2,1)}, bf16[2,2,128,256]{3,2,1,0:T(8,128)(2,1)}, u32[]{:S(2)}, u32[]{:S(2)}) collective-permute-start(bf16[2,2,128,256]{3,2,1,0:T(8,128)(2,1)} %fusion.40), channel_id=1, source_target_pairs={{0,31},{1,0},{2,1},{3,2},{4,3},{5,4},{6,5},{7,6},{8,7},{9,8},{10,9... | collective-permute-start | bytes 786440 | tf_op jit(solution)/shard_map/ppermute | solution.py:10
  19.7 2.8 %copy.22 = bf16[2,2,1536,256]{2,3,1,0:T(8,128)(2,1)} copy(bf16[2,2,1536,256]{3,2,1,0:T(8,128)(2,1)S(1)} %copy-done) | data formatting | bytes 6291456 | tf_op args[0]
  22.5 1.1 copy.23
  23.6 0.3 collective-permute-done.1
  23.9 1.1 copy.24
  25.1 10.3 %fusion.29 = bf16[2,2,256,4,512]{4,2,3,1,0:T(8,128)(2,1)S(1)} fusion(s32[4,512]{1,0:T(4,128)S(1)} %copy-done.5, bf16[2,2,128,256]{2,3,1,0:T(8,128)(2,1)S(1)} %copy.24, bf16[2,2,128,256]{2,3,1,0:T(8,128)(2,1)S(1)} %copy.23, bf16[2,2,1536,256]{2,3,1,0:T(8,128)(2,1)} %copy.22), kind=kOutput, calls=%fused_computation.30 | convolution fusion | flops 7532969984 | bytes 7872512 | tf_op jit(solution)/shard_map/pne,wqer->wqpnr/dot_general | solution.py:45
  35.4 2.0 copy-done.6
  37.4 1.3 fusion.36
  38.8 3.9 %fusion.68 = f32[64,2,32,256]{3,0,2,1:T(8,128)} fusion(f32[4,2,32,256]{3,2,1,0:T(8,128)S(1)} %fusion.36, s32[4]{0:T(128)S(1)} %copy-done.4), kind=kOutput, calls=%fused_computation.60 | convolution fusion | flops 50331904 | bytes 4456464 | tf_op jit(solution)/shard_map/pb,pwcr->bwcr/dot_general | solution.py:53
  42.7 0.4 reshape.11
  43.0 28.0 %reshape.10 = bf16[4,2,2,512,2,512]{5,4,3,2,1,0:T(2,128)(2,1)} reshape(bf16[4,2,1024,1024]{3,2,1,0:T(8,128)(2,1)} %param.8) | data formatting | bytes 33554432 | tf_op jit(solution)/shard_map/reshape | solution.py:67
  71.1 9.2 %all_gather.3 = bf16[64,2,32,32]{3,2,1,0:T(8,128)(2,1)S(1)} all-gather(bf16[16,2,32,32]{3,2,1,0:T(8,128)(2,1)S(1)} %copy-done.3), channel_id=1, replica_groups=mesh['patch'=8,'coarse'=4] {'coarse'}, dimensions={0}, use_global_device_ids=true | all-gather | bytes 327680 | tf_op jit(solution)/shard_map/all_gather | solution.py:57
  80.3 15.3 %fusion = f32[2,4,256,2,512,1]{4,2,5,3,1,0:T(8,128)} fusion(bf16[4,2,2,512,2,512]{5,4,3,2,1,0:T(2,128)(2,1)} %reshape.10, bf16[2,2,256,4,512]{4,2,3,1,0:T(8,128)(2,1)} %copy-done.6), kind=kOutput, calls=%fused_computation | convolution fusion | flops 4294967296 | bytes 29360128 | tf_op jit(solution)/shard_map/pwabqn,wqpnr->wapbr/dot_general | solution.py:68
  95.6 91.1 %all-reduce.2.cloned.1.call-done = f32[64,2,32,256]{3,0,2,1:T(8,128)} async-done(((f32[64,2,32,256]{3,0,2,1:T(8,128)}), f32[64,2,32,256]{3,0,2,1:T(8,128)}) %all-reduce.2.cloned.1.call-update) | async-done | bytes 4194320 | tf_op jit(solution)/shard_map/psum | solution.py:56
  186.7 7.1 %convert_bitcast_fusion = bf16[64,2,32,256]{3,2,1,0:T(8,128)(2,1)S(1)} fusion(bf16[64,2,32,32]{3,2,1,0:T(8,128)(2,1)S(1)} %all_gather.3, f32[64,2,32,256]{3,0,2,1:T(8,128)} %all-reduce.2.cloned.1.call-done), kind=kOutput, calls=%fused_computation.33 | convolution fusion | flops 403701760 | bytes 6553600 | tf_op jit(solution)/shard_map/bwcd,bwdr->bwcr/dot_general | solution.py:58
  193.8 1.2 fusion.44
  195.0 1.3 fusion.60
  196.3 3.2 %copy-done.1 = f32[2,4,256,2,512]{4,2,3,1,0:T(8,128)} copy-done((f32[2,4,256,2,512]{4,2,3,1,0:T(8,128)}, f32[2,4,256,2,512]{4,2,3,1,0:T(8,128)S(1)}, u32[]{:S(2)}) %copy-start.1) | copy-done | bytes 8388632
  199.5 13.1 %fusion.4 = f32[2,2,256,1792,1]{3,2,1,4,0:T(8,128)} fusion(s32[4,512]{1,0:T(4,128)S(1)} %copy-done.5, f32[2,4,256,2,512]{4,2,3,1,0:T(8,128)S(1)} %fusion.60, f32[2,4,256,2,512,1]{4,2,5,3,1,0:T(8,128)} %fusion), kind=kOutput, calls=%fused_computation.5 | convolution fusion | flops 7530348544 | bytes 24125440 | tf_op jit(solution)/shard_map/pne,wqpnr->wqer/dot_general | solution.py:17
  212.6 18.2 %fusion.78 = (bf16[2,2,1792,256]{2,3,1,0:T(8,128)(2,1)S(1)}, f32[2,2,1792,256]{2,3,1,0:T(8,128)}) fusion(f32[2,2,256,1792,1]{3,2,1,4,0:T(8,128)} %fusion.4, s32[4,512]{1,0:T(4,128)S(1)} %copy-done.5, f32[2,4,256,2,512]{4,2,3,1,0:T(8,128)} %copy-done.1, f32[2,4,256,2,512,1]{4,2,5,3,1,0:T(8,128)} %fusion), kind=kOutput, calls=%fused_computation.71 | convolution fusion | flops 7527727104 | bytes 35135488 | tf_op jit(solution)/shard_map/pne,wqpnr->wqer/dot_general | solution.py:16
  230.9 0.9 collective-permute-start.2
  231.8 3.9 %collective-permute-done.2 = bf16[2,2,128,256]{2,3,1,0:T(8,128)(2,1)S(1)} collective-permute-done((bf16[2,2,128,256]{2,3,1,0:T(8,128)(2,1)S(1)}, bf16[2,2,128,256]{2,3,1,0:T(8,128)(2,1)S(1)}, u32[]{:S(2)}, u32[]{:S(2)}) %collective-permute-start.2) | collective-permute-done | bytes 262176 | tf_op jit(solution)/shard_map/ppermute | solution.py:10
  235.7 1.1 fusion.48
  236.8 1.1 fusion.50
  237.9 3.3 %collective-permute-done.3 = bf16[2,2,128,256]{2,3,1,0:T(8,128)(2,1)S(1)} collective-permute-done((bf16[2,2,128,256]{2,3,1,0:T(8,128)(2,1)S(1)}, bf16[2,2,128,256]{2,3,1,0:T(8,128)(2,1)S(1)}, u32[]{:S(2)}, u32[]{:S(2)}) %collective-permute-start.3) | collective-permute-done | bytes 262176 | tf_op jit(solution)/shard_map/ppermute | solution.py:10
  241.2 1.1 fusion.54
  242.3 4.2 %fusion.16 = bf16[2,2,1536,256]{2,3,1,0:T(8,128)(2,1)S(1)} fusion(f32[2,2,1792,256]{2,3,1,0:T(8,128)} %get-tuple-element.10, f32[2,2,256,1536]{3,2,1,0:T(8,128)S(1)} %fusion.54, f32[2,2,256,1536]{3,2,1,0:T(8,128)S(1)} %fusion.50, f32[2,2,256,1536]{3,2,1,0:T(8,128)S(1)} %fusion.48, bf16[2,2,128,256]{2,3,1,0:T(8,128)(2,1)S(1)} %collective-permute-done.3, ...), kind=kOutput, calls=%fused_computation.19 | convolution fusion | flops 410714112 | bytes 28574208 | tf_op jit(solution)/shard_map/kn,wqkr->wqnr/dot_general | solution.py:16
  246.5 2.8 %copy.36 = bf16[2,2,1536,256]{3,2,1,0:T(8,128)(2,1)} copy(bf16[2,2,1536,256]{2,3,1,0:T(8,128)(2,1)S(1)} %fusion.16) | data formatting | bytes 6291456 | tf_op jit(solution)/shard_map/convert_element_type | solution.py:86
  (17 shorter events, 0.1 us)
Async XLA Ops:
  6.5 13.2 %copy-start = (bf16[2,2,1536,256]{3,2,1,0:T(8,128)(2,1)S(1)}, bf16[2,2,1536,256]{3,2,1,0:T(8,128)(2,1)}, u32[]{:S(2)}) copy-start(bf16[2,2,1536,256]{3,2,1,0:T(8,128)(2,1)} %param.7) | copy-start | bytes 9437188
  6.5 180.1 %all-reduce.2.cloned.1.call-start = ((), (), s32[]{:S(2)}) async-start(), calls=%async_computation | async-start | bytes 8388608 | tf_op jit(solution)/shard_map/psum | solution.py:56
  10.0 12.5 %collective-permute-start = (bf16[2,2,128,256]{3,2,1,0:T(8,128)(2,1)S(1)}, bf16[2,2,128,256]{3,2,1,0:T(8,128)(2,1)}, u32[]{:S(2)}, u32[]{:S(2)}) collective-permute-start(bf16[2,2,128,256]{3,2,1,0:T(8,128)(2,1)S(1)} %fusion.39), channel_id=1, source_target_pairs={{0,1},{1,2},{2,3},{3,4},{4,5},{5,6},{6,7},{7,8},{8,9},{9,10},{10,1... | collective-permute-start | bytes 786440 | tf_op jit(solution)/shard_map/ppermute | solution.py:10
  13.8 11.3 %copy-start.5 = (s32[4,512]{1,0:T(4,128)S(1)}, s32[4,512]{1,0:T(4,128)}, u32[]{:S(2)}) copy-start(s32[4,512]{1,0:T(4,128)} %param.11) | copy-start | bytes 24580
  13.8 10.1 %collective-permute-start.1 = (bf16[2,2,128,256]{3,2,1,0:T(8,128)(2,1)}, bf16[2,2,128,256]{3,2,1,0:T(8,128)(2,1)}, u32[]{:S(2)}, u32[]{:S(2)}) collective-permute-start(bf16[2,2,128,256]{3,2,1,0:T(8,128)(2,1)} %fusion.40), channel_id=1, source_target_pairs={{0,31},{1,0},{2,1},{3,2},{4,3},{5,4},{6,5},{7,6},{8,7},{9,8},{10,9... | collective-permute-start | bytes 786440 | tf_op jit(solution)/shard_map/ppermute | solution.py:10
  25.1 12.4 %copy-start.2 = (bf16[4,2,1024,32]{2,3,1,0:T(8,128)(2,1)S(1)}, bf16[4,2,1024,32]{2,3,1,0:T(8,128)(2,1)}, u32[]{:S(2)}) copy-start(bf16[4,2,1024,32]{2,3,1,0:T(8,128)(2,1)} %param.9) | copy-start | bytes 1572868
  35.4 2.1 copy-start.6
  35.4 3.4 %copy-start.4 = (s32[4]{0:T(128)S(1)}, s32[4]{0:T(128)}, u32[]{:S(2)}) copy-start(s32[4]{0:T(128)} %param.13) | copy-start | bytes 52
  43.0 28.0 %copy-start.3 = (bf16[16,2,32,32]{3,2,1,0:T(8,128)(2,1)S(1)}, bf16[16,2,32,32]{3,2,1,0:T(8,128)(2,1)}, u32[]{:S(2)}) copy-start(bf16[16,2,32,32]{3,2,1,0:T(8,128)(2,1)} %param.10) | copy-start | bytes 196612
  196.3 3.2 %copy-start.1 = (f32[2,4,256,2,512]{4,2,3,1,0:T(8,128)}, f32[2,4,256,2,512]{4,2,3,1,0:T(8,128)S(1)}, u32[]{:S(2)}) copy-start(f32[2,4,256,2,512]{4,2,3,1,0:T(8,128)S(1)} %fusion.60) | copy-start | bytes 25165828
  230.9 4.8 %collective-permute-start.2 = (bf16[2,2,128,256]{2,3,1,0:T(8,128)(2,1)S(1)}, bf16[2,2,128,256]{2,3,1,0:T(8,128)(2,1)S(1)}, u32[]{:S(2)}, u32[]{:S(2)}) collective-permute-start(bf16[2,2,128,256]{2,3,1,0:T(8,128)(2,1)S(1)} %get-tuple-element.5), channel_id=1, source_target_pairs={{0,31},{1,0},{2,1},{3,2},{4,3},{5,4},{6,5},{7,6},{8,7},{9,8},{10,9... | collective-permute-start | bytes 786440 | tf_op jit(solution)/shard_map/ppermute | solution.py:10
  231.8 9.4 %collective-permute-start.3 = (bf16[2,2,128,256]{2,3,1,0:T(8,128)(2,1)S(1)}, bf16[2,2,128,256]{2,3,1,0:T(8,128)(2,1)S(1)}, u32[]{:S(2)}, u32[]{:S(2)}) collective-permute-start(bf16[2,2,128,256]{2,3,1,0:T(8,128)(2,1)S(1)} %get-tuple-element.6), channel_id=1, source_target_pairs={{0,1},{1,2},{2,3},{3,4},{4,5},{5,6},{6,7},{7,8},{8,9},{9,10},{10,1... | collective-permute-start | bytes 786440 | tf_op jit(solution)/shard_map/ppermute | solution.py:10
Sparse Core Ops, SparseCore 0:
  42.8 143.8 all-reduce.1
where the time goes:
time: 257 us; the launch traced here: 256 us
  waiting for transfers between devices  98.6 us (38%)
  matrix products  84.9 us (33%)
  local copies, waits for them, and re-layouts  42.4 us (16%)
  between operations  13.5 us (5%)
  blocking collectives  9.23 us (4%)
  starting transfers between devices  7.39 us (3%)
    psum x1, waiting for transfers between devices, per_device(): totals = lax.psum(partial_sums, ('patch', 'coarse'))  91.1 us
    reshape x1, local copies, waits for them, and re-layouts, per_device(): patch_inv.reshape(patches, wave_count, 2, patch_nodes, 2, patch_nodes)  28 us
    dot_general x3, matrix products, spread_rows(): jnp.einsum(form, selector, upper_part, preferred_element_type=jnp.float32)  23.4 us
    dot_general x1, matrix products, per_device(): jnp.einsum('pwabqn,wqpnr->wapbr', inverse, gathered, preferred_element_ty...  15.3 us
    dot_general x3, matrix products, spread_rows(): jnp.einsum(form, selector, lower_part, preferred_element_type=jnp.float32)  15.3 us
    dot_general x1, matrix products, per_device(): jnp.einsum('pne,wqer->wqpnr', ext_select, extended, preferred_element_typ...  10.3 us
    all_gather x1, blocking collectives, per_device(): inverses = lax.all_gather(coarse_inv, 'coarse', axis=0, tiled=True)  9.23 us
    unnamed x15, local copies, waits for them, and re-layouts  8.05 us
  transfers between devices with their start and end apart: 5, of which 4 were waited for; matrix products, arithmetic and copies ran while one was open for 21% of the time, Pallas kernels for 0%

commit v1 on v0

--- a/solution.py
+++ b/solution.py
@@ -53,7 +53,7 @@
     partial_sums = jnp.einsum(
         "pb,pwcr->bwcr", member.astype(jnp.float32), restricted, precision=highest
     )
-    totals = lax.psum(partial_sums, ("patch", "coarse"))
+    totals = lax.psum(lax.psum(partial_sums, "coarse"), "patch")
     inverses = lax.all_gather(coarse_inv, "coarse", axis=0, tiled=True)
     coarse_coef = jnp.einsum(
         "bwcd,bwdr->bwcr", inverses.astype(jnp.float32), totals, precision=highest

time: 257 us -> 362 us (1.41)
  waiting for transfers between devices: 98.6 us -> 202 us
    psum x1 -> x2, waiting for transfers between devices: 91.1 us -> 194 us  [per_device(): totals = lax.psum(lax.psum(partial_sums, 'coarse'), 'patch')]
  transfers between devices with their start and end apart: 5 -> 6, of which waited for: 4 -> 5; matrix products, arithmetic and copies ran while one was open for 21% -> 15% of each run, Pallas kernels for 0% -> 0%
where the time goes in v1:
time: 362 us; the launch traced here: 361 us
  waiting for transfers between devices  202 us (56%)
  matrix products  84.8 us (23%)
  local copies, waits for them, and re-layouts  42.3 us (12%)
  between operations  13.5 us (4%)
  blocking collectives  9.41 us (3%)
  starting transfers between devices  9.1 us (3%)
    psum x2, waiting for transfers between devices, per_device(): totals = lax.psum(lax.psum(partial_sums, 'coarse'), 'patch')  194 us
    reshape x1, local copies, waits for them, and re-layouts, per_device(): patch_inv.reshape(patches, wave_count, 2, patch_nodes, 2, patch_nodes)  28.1 us
    dot_general x3, matrix products, spread_rows(): jnp.einsum(form, selector, upper_part, preferred_element_type=jnp.float32)  23.4 us
    dot_general x3, matrix products, spread_rows(): jnp.einsum(form, selector, lower_part, preferred_element_type=jnp.float32)  15.3 us
    dot_general x1, matrix products, per_device(): jnp.einsum('pwabqn,wqpnr->wapbr', inverse, gathered, preferred_element_ty...  15.2 us
    dot_general x1, matrix products, per_device(): jnp.einsum('pne,wqer->wqpnr', ext_select, extended, preferred_element_typ...  10.3 us
    all_gather x1, blocking collectives, per_device(): inverses = lax.all_gather(coarse_inv, 'coarse', axis=0, tiled=True)  9.41 us
    ppermute x4, starting transfers between devices, passed_along(): return lax.ppermute(value, axis, pairs)  9.06 us
  transfers between devices with their start and end apart: 6, of which 5 were waited for; matrix products, arithmetic and copies ran while one was open for 15% of the time, Pallas kernels for 0%

profile of v1, /device:TPU:0, one launch (start us, length us, event | category | flops | bytes accessed | tf_op | source)
XLA Modules:
  0.0 360.8 jit_solution(7779572696223923256)
XLA Ops:
  6.5 0.8 slice_bitcast_fusion.1
  7.4 2.6 fusion.39
  10.0 0.5 collective-permute-start
  10.6 3.2 fusion.40
  13.8 5.9 %collective-permute-start.1 = (bf16[2,2,128,256]{3,2,1,0:T(8,128)(2,1)}, bf16[2,2,128,256]{3,2,1,0:T(8,128)(2,1)}, u32[]{:S(2)}, u32[]{:S(2)}) collective-permute-start(bf16[2,2,128,256]{3,2,1,0:T(8,128)(2,1)} %fusion.40), channel_id=1, source_target_pairs={{0,31},{1,0},{2,1},{3,2},{4,3},{5,4},{6,5},{7,6},{8,7},{9,8},{10,9... | collective-permute-start | bytes 786440 | tf_op jit(solution)/shard_map/ppermute | solution.py:10
  19.7 2.8 copy.22
  22.5 1.1 copy.23
  23.9 1.1 copy.24
  25.1 10.3 %fusion.29 = bf16[2,2,256,4,512]{4,2,3,1,0:T(8,128)(2,1)S(1)} fusion(s32[4,512]{1,0:T(4,128)S(1)} %copy-done.5, bf16[2,2,128,256]{2,3,1,0:T(8,128)(2,1)S(1)} %copy.24, bf16[2,2,128,256]{2,3,1,0:T(8,128)(2,1)S(1)} %copy.23, bf16[2,2,1536,256]{2,3,1,0:T(8,128)(2,1)} %copy.22), kind=kOutput, calls=%fused_computation.30 | convolution fusion | flops 7532969984 | bytes 7872512 | tf_op jit(solution)/shard_map/pne,wqer->wqpnr/dot_general | solution.py:45
  35.4 1.9 copy-done.6
  37.3 1.3 fusion.36
  38.6 3.9 %fusion.68 = f32[64,2,32,256]{3,0,2,1:T(8,128)} fusion(f32[4,2,32,256]{3,2,1,0:T(8,128)S(1)} %fusion.36, s32[4]{0:T(128)S(1)} %copy-done.4), kind=kOutput, calls=%fused_computation.60 | convolution fusion | flops 50331904 | bytes 4456464 | tf_op jit(solution)/shard_map/pb,pwcr->bwcr/dot_general | solution.py:53
  42.6 86.9 %all-reduce.3.cloned.1.call-done = f32[64,2,32,256]{3,0,2,1:T(8,128)} async-done(((f32[64,2,32,256]{3,0,2,1:T(8,128)}), f32[64,2,32,256]{3,0,2,1:T(8,128)}) %all-reduce.3.cloned.1.call-update) | async-done | bytes 4194320 | tf_op jit(solution)/shard_map/psum | solution.py:56
  129.5 0.4 reshape.11
  129.9 28.1 %reshape.10 = bf16[4,2,2,512,2,512]{5,4,3,2,1,0:T(2,128)(2,1)} reshape(bf16[4,2,1024,1024]{3,2,1,0:T(8,128)(2,1)} %param.8) | data formatting | bytes 33554432 | tf_op jit(solution)/shard_map/reshape | solution.py:67
  158.0 9.4 %all_gather.3 = bf16[64,2,32,32]{3,2,1,0:T(8,128)(2,1)S(1)} all-gather(bf16[16,2,32,32]{3,2,1,0:T(8,128)(2,1)S(1)} %copy-done.3), channel_id=1, replica_groups=mesh['patch'=8,'coarse'=4] {'coarse'}, dimensions={0}, use_global_device_ids=true | all-gather | bytes 327680 | tf_op jit(solution)/shard_map/all_gather | solution.py:57
  167.4 15.2 %fusion = f32[2,4,256,2,512,1]{4,2,5,3,1,0:T(8,128)} fusion(bf16[4,2,2,512,2,512]{5,4,3,2,1,0:T(2,128)(2,1)} %reshape.10, bf16[2,2,256,4,512]{4,2,3,1,0:T(8,128)(2,1)} %copy-done.6), kind=kOutput, calls=%fused_computation | convolution fusion | flops 4294967296 | bytes 29360128 | tf_op jit(solution)/shard_map/pwabqn,wqpnr->wapbr/dot_general | solution.py:68
  182.6 107.2 %all-reduce.5.cloned.1.call-done = f32[64,2,32,256]{3,0,2,1:T(8,128)} async-done(((f32[64,2,32,256]{3,0,2,1:T(8,128)}), f32[64,2,32,256]{3,0,2,1:T(8,128)}) %all-reduce.5.cloned.1.call-update) | async-done | bytes 4194320 | tf_op jit(solution)/shard_map/psum | solution.py:56
  289.8 7.1 %convert_bitcast_fusion = bf16[64,2,32,256]{3,2,1,0:T(8,128)(2,1)S(1)} fusion(bf16[64,2,32,32]{3,2,1,0:T(8,128)(2,1)S(1)} %all_gather.3, f32[64,2,32,256]{3,0,2,1:T(8,128)} %all-reduce.5.cloned.1.call-done), kind=kOutput, calls=%fused_computation.33 | convolution fusion | flops 403701760 | bytes 6553600 | tf_op jit(solution)/shard_map/bwcd,bwdr->bwcr/dot_general | solution.py:58
  296.9 1.2 fusion.44
  298.1 1.3 fusion.60
  299.4 3.2 copy-done.1
  302.6 13.1 %fusion.4 = f32[2,2,256,1792,1]{3,2,1,4,0:T(8,128)} fusion(s32[4,512]{1,0:T(4,128)S(1)} %copy-done.5, f32[2,4,256,2,512]{4,2,3,1,0:T(8,128)S(1)} %fusion.60, f32[2,4,256,2,512,1]{4,2,5,3,1,0:T(8,128)} %fusion), kind=kOutput, calls=%fused_computation.5 | convolution fusion | flops 7530348544 | bytes 24125440 | tf_op jit(solution)/shard_map/pne,wqpnr->wqer/dot_general | solution.py:17
  315.7 18.2 %fusion.78 = (bf16[2,2,1792,256]{2,3,1,0:T(8,128)(2,1)S(1)}, f32[2,2,1792,256]{2,3,1,0:T(8,128)}) fusion(f32[2,2,256,1792,1]{3,2,1,4,0:T(8,128)} %fusion.4, s32[4,512]{1,0:T(4,128)S(1)} %copy-done.5, f32[2,4,256,2,512]{4,2,3,1,0:T(8,128)} %copy-done.1, f32[2,4,256,2,512,1]{4,2,5,3,1,0:T(8,128)} %fusion), kind=kOutput, calls=%fused_computation.71 | convolution fusion | flops 7527727104 | bytes 35135488 | tf_op jit(solution)/shard_map/pne,wqpnr->wqer/dot_general | solution.py:16
  334.0 2.6 collective-permute-start.2
  336.6 3.9 %collective-permute-done.2 = bf16[2,2,128,256]{2,3,1,0:T(8,128)(2,1)S(1)} collective-permute-done((bf16[2,2,128,256]{2,3,1,0:T(8,128)(2,1)S(1)}, bf16[2,2,128,256]{2,3,1,0:T(8,128)(2,1)S(1)}, u32[]{:S(2)}, u32[]{:S(2)}) %collective-permute-start.2) | collective-permute-done | bytes 262176 | tf_op jit(solution)/shard_map/ppermute | solution.py:10
  340.5 1.1 fusion.48
  341.6 1.1 fusion.50
  342.6 3.3 collective-permute-done.3
  346.0 1.1 fusion.54
  347.1 4.2 %fusion.16 = bf16[2,2,1536,256]{2,3,1,0:T(8,128)(2,1)S(1)} fusion(f32[2,2,1792,256]{2,3,1,0:T(8,128)} %get-tuple-element.10, f32[2,2,256,1536]{3,2,1,0:T(8,128)S(1)} %fusion.54, f32[2,2,256,1536]{3,2,1,0:T(8,128)S(1)} %fusion.50, f32[2,2,256,1536]{3,2,1,0:T(8,128)S(1)} %fusion.48, bf16[2,2,128,256]{2,3,1,0:T(8,128)(2,1)S(1)} %collective-permute-done.3, ...), kind=kOutput, calls=%fused_computation.19 | convolution fusion | flops 410714112 | bytes 28574208 | tf_op jit(solution)/shard_map/kn,wqkr->wqnr/dot_general | solution.py:16
  351.2 2.8 copy.36
  (20 shorter events, 0.5 us)
Async XLA Ops:
  6.5 13.2 %copy-start = (bf16[2,2,1536,256]{3,2,1,0:T(8,128)(2,1)S(1)}, bf16[2,2,1536,256]{3,2,1,0:T(8,128)(2,1)}, u32[]{:S(2)}) copy-start(bf16[2,2,1536,256]{3,2,1,0:T(8,128)(2,1)} %param.7) | copy-start | bytes 9437188
  6.5 123.0 %all-reduce.3.cloned.1.call-start = ((), (), s32[]{:S(2)}) async-start(), calls=%async_computation | async-start | bytes 8388608 | tf_op jit(solution)/shard_map/psum | solution.py:56
  10.0 12.5 %collective-permute-start = (bf16[2,2,128,256]{3,2,1,0:T(8,128)(2,1)S(1)}, bf16[2,2,128,256]{3,2,1,0:T(8,128)(2,1)}, u32[]{:S(2)}, u32[]{:S(2)}) collective-permute-start(bf16[2,2,128,256]{3,2,1,0:T(8,128)(2,1)S(1)} %fusion.39), channel_id=1, source_target_pairs={{0,1},{1,2},{2,3},{3,4},{4,5},{5,6},{6,7},{7,8},{8,9},{9,10},{10,1... | collective-permute-start | bytes 786440 | tf_op jit(solution)/shard_map/ppermute | solution.py:10
  13.8 11.3 %copy-start.5 = (s32[4,512]{1,0:T(4,128)S(1)}, s32[4,512]{1,0:T(4,128)}, u32[]{:S(2)}) copy-start(s32[4,512]{1,0:T(4,128)} %param.11) | copy-start | bytes 24580
  13.8 10.1 %collective-permute-start.1 = (bf16[2,2,128,256]{3,2,1,0:T(8,128)(2,1)}, bf16[2,2,128,256]{3,2,1,0:T(8,128)(2,1)}, u32[]{:S(2)}, u32[]{:S(2)}) collective-permute-start(bf16[2,2,128,256]{3,2,1,0:T(8,128)(2,1)} %fusion.40), channel_id=1, source_target_pairs={{0,31},{1,0},{2,1},{3,2},{4,3},{5,4},{6,5},{7,6},{8,7},{9,8},{10,9... | collective-permute-start | bytes 786440 | tf_op jit(solution)/shard_map/ppermute | solution.py:10
  25.1 12.3 %copy-start.2 = (bf16[4,2,1024,32]{2,3,1,0:T(8,128)(2,1)S(1)}, bf16[4,2,1024,32]{2,3,1,0:T(8,128)(2,1)}, u32[]{:S(2)}) copy-start(bf16[4,2,1024,32]{2,3,1,0:T(8,128)(2,1)} %param.9) | copy-start | bytes 1572868
  35.4 1.9 copy-start.6
  35.4 3.2 copy-start.4
  42.5 247.2 %all-reduce.5.cloned.1.call-start = ((), (), s32[]{:S(2)}) async-start(), calls=%async_computation.1 | async-start | bytes 8388608 | tf_op jit(solution)/shard_map/psum | solution.py:56
  129.9 28.1 %copy-start.3 = (bf16[16,2,32,32]{3,2,1,0:T(8,128)(2,1)S(1)}, bf16[16,2,32,32]{3,2,1,0:T(8,128)(2,1)}, u32[]{:S(2)}) copy-start(bf16[16,2,32,32]{3,2,1,0:T(8,128)(2,1)} %param.10) | copy-start | bytes 196612
  299.4 3.2 copy-start.1
  334.0 6.5 %collective-permute-start.2 = (bf16[2,2,128,256]{2,3,1,0:T(8,128)(2,1)S(1)}, bf16[2,2,128,256]{2,3,1,0:T(8,128)(2,1)S(1)}, u32[]{:S(2)}, u32[]{:S(2)}) collective-permute-start(bf16[2,2,128,256]{2,3,1,0:T(8,128)(2,1)S(1)} %get-tuple-element.5), channel_id=1, source_target_pairs={{0,31},{1,0},{2,1},{3,2},{4,3},{5,4},{6,5},{7,6},{8,7},{9,8},{10,9... | collective-permute-start | bytes 786440 | tf_op jit(solution)/shard_map/ppermute | solution.py:10
  336.6 9.4 %collective-permute-start.3 = (bf16[2,2,128,256]{2,3,1,0:T(8,128)(2,1)S(1)}, bf16[2,2,128,256]{2,3,1,0:T(8,128)(2,1)S(1)}, u32[]{:S(2)}, u32[]{:S(2)}) collective-permute-start(bf16[2,2,128,256]{2,3,1,0:T(8,128)(2,1)S(1)} %get-tuple-element.6), channel_id=1, source_target_pairs={{0,1},{1,2},{2,3},{3,4},{4,5},{5,6},{6,7},{7,8},{8,9},{9,10},{10,1... | collective-permute-start | bytes 786440 | tf_op jit(solution)/shard_map/ppermute | solution.py:10
Sparse Core Ops, SparseCore 0:
  42.7 86.7 all-reduce.2
  133.2 156.5 all-reduce.4
